TPU v7x, 256 devices: a whole 4x4x8 slice. The times are simulated.
256 devices in a mesh: rows: 32 (over y, x, core), cols: 8 (over z).
Axes of the slice: x: 4, y: 4, z: 8, core: 2. Of those that a mesh axis runs over, the one named last changes fastest.
Arguments:
- anomalies: bfloat16 [131072, 64], P(('rows', 'cols')), may hold values from -6 to 6
- innovations: bfloat16 [131072, 64], P(('rows', 'cols')), may hold values from -3 to 3
- pair_rows: int32 [32, 8192], P('rows', 'cols'), may hold values from 0 to 31, as said below
- pair_cols: int32 [32, 8192], P('rows', 'cols'), may hold values from 0 to 127
- pair_dist: int32 [32, 8192], P('rows', 'cols'), may hold values from 0 to 7
- pair_counts: int32 [32, 8], P('rows', 'cols'), may hold values from 128 to 1024, as said below
Outputs:
- increment: float32 [131072, 64], P(('rows', 'cols'))
Inputs may be any that keep to these rules, and one draw needn't show every extreme that they name: In the 1024 slots of one device the pairs (pair_rows, pair_cols) are distinct, and each row block stands in at most 32 of them. `pair_counts`: some device has all its slots live in every draw.
All inputs are finite; a program needn't handle non-finite values.
Results may differ from a plain program's by a relative error of at most 0.005.
Values may be sent and summed in bfloat16 or wider, within the bound.
A program may use at most 128 MiB of HBM per device.

v0:
```python
import math

import jax
import jax.numpy as jnp
from jax import lax
from jax.sharding import PartitionSpec as P

BLK = 128
M = 64
TAPER_CELLS = 8


DIST_SCALE = 4.0


def local(anomalies, innovations, pair_rows, pair_cols, pair_dist, pair_counts):
    cell_dev = anomalies.shape[0]
    members = anomalies.shape[1]
    columns = innovations.shape[1]
    row_count = lax.axis_size("rows")
    col_count = lax.axis_size("cols")
    everything = lax.all_gather(anomalies, ("rows", "cols"), axis=0, tiled=True)
    col_innov = lax.all_gather(innovations, "rows", axis=0, tiled=True)
    all_cells = everything.reshape(row_count, col_count, cell_dev, members)
    row_anom = lax.dynamic_index_in_dim(all_cells, lax.axis_index("rows"), 0, keepdims=False)
    row_anom = row_anom.reshape(col_count * cell_dev, members)
    col_anom = lax.dynamic_index_in_dim(all_cells, lax.axis_index("cols"), 1, keepdims=False)
    col_anom = col_anom.reshape(row_count * cell_dev, members)
    row_blocks = row_anom.reshape(-1, BLK, members)
    col_blocks = col_anom.reshape(-1, BLK, members)
    innov_blocks = col_innov.reshape(-1, BLK, columns)
    block_total = row_blocks.shape[0]
    slots = pair_rows.shape[1]
    group_size = math.gcd(128, slots)
    offsets = jnp.arange(BLK)
    kernel = jnp.exp(
        -jnp.abs(offsets[:, None] - offsets[None, :]).astype(jnp.float32) / TAPER_CELLS
    )
    block_index = jnp.arange(block_total)
    slot_offsets = jnp.arange(group_size)
    filled = pair_counts[0, 0]
    loop_turns = (filled + group_size - 1) // group_size
    row_list = pair_rows[0]
    col_list = pair_cols[0]
    dist_list = pair_dist[0]

    def one_group(turn_index, totals):
        first_slot = turn_index * group_size
        local_rows = lax.dynamic_slice_in_dim(row_list, first_slot, group_size)
        col_local = lax.dynamic_slice_in_dim(col_list, first_slot, group_size)
        distances = lax.dynamic_slice_in_dim(dist_list, first_slot, group_size)
        live_slot = first_slot + slot_offsets < filled
        left = jnp.take(row_blocks, local_rows, axis=0)
        right = jnp.take(col_blocks, col_local, axis=0)
        innov = jnp.take(innov_blocks, col_local, axis=0)
        products = jnp.einsum("pim,pjm->pij", left, right, preferred_element_type=jnp.float32)
        block_weight = jnp.where(
            live_slot, jnp.exp(-distances.astype(jnp.float32) / DIST_SCALE), 0.0
        )
        tapered = (products * (1.0 / (M - 1)) * block_weight[:, None, None] * kernel).astype(
            jnp.bfloat16
        )
        applied = jnp.einsum("pij,pjk->pik", tapered, innov, preferred_element_type=jnp.float32)
        onehot = (local_rows[:, None] == block_index[None, :]).astype(jnp.float32)
        return totals + jnp.einsum("pr,pik->rik", onehot, applied)

    totals = jnp.zeros((block_total, BLK, columns), jnp.float32)
    totals = lax.fori_loop(0, loop_turns, one_group, totals)
    partial_rows = totals.reshape(block_total * BLK, columns)
    return lax.psum_scatter(partial_rows, "cols", scatter_dimension=0, tiled=True)


def solution(mesh):
    in_specs = (
        P(("rows", "cols"), None),
        P(("rows", "cols"), None),
        P("rows", "cols"),
        P("rows", "cols"),
        P("rows", "cols"),
        P("rows", "cols"),
    )
    out_specs = P(("rows", "cols"), None)
    return jax.shard_map(local, mesh=mesh, in_specs=in_specs, out_specs=out_specs, check_vma=False)
```

profile of v0, /device:TPU:1, one launch (start us, length us, event | category | flops | bytes accessed | tf_op | source)
XLA Modules:
  0.0 501.4 jit_solution(640628253102442215)
XLA Ops:
  8.7 55.1 %all-gather.5.cloned.1.call-done = bf16[16384,64]{0,1:T(8,128)(2,1)} async-done(((bf16[512,64]{0,1:T(8,128)(2,1)}), bf16[16384,64]{0,1:T(8,128)(2,1)}) %all-gather.5.cloned.1.call-update) | async-done | bytes 2097168 | tf_op jit(solution)/shard_map/all_gather | solution.py:23
  63.8 4.8 copy.9
  68.6 128.4 %all-gather.3.cloned.1.call-done = bf16[131072,64]{0,1:T(8,128)(2,1)} async-done(((bf16[512,64]{0,1:T(8,128)(2,1)}), bf16[131072,64]{0,1:T(8,128)(2,1)}) %all-gather.3.cloned.1.call-update) | async-done | bytes 16777232 | tf_op jit(solution)/shard_map/all_gather | solution.py:22
  197.0 12.0 %copy.13 = bf16[8,8,256,512]{3,2,1,0:T(8,128)(2,1)S(1)} copy(bf16[8,8,256,512]{3,1,2,0:T(8,128)(2,1)} %bitcast.30) | data formatting | bytes 33554432
  209.0 5.7 %copy-done = bf16[8,8,256,512]{3,2,1,0:T(8,128)(2,1)} copy-done((bf16[8,8,256,512]{3,2,1,0:T(8,128)(2,1)}, bf16[8,8,256,512]{3,2,1,0:T(8,128)(2,1)S(1)}, u32[]{:S(2)}) %copy-start) | copy-done | bytes 16777240
  214.7 5.3 %constant_dynamic-slice_fusion = bf16[32,1,512,64]{2,1,0,3:T(2,128)(2,1)} fusion(bf16[32,8,512,64]{2,1,0,3:T(8,128)(2,1)S(1)} %bitcast.28, s32[]{:T(128)S(6)} %select_n.39), kind=kLoop, calls=%fused_computation.36 | loop fusion | bytes 4194308 | tf_op jit(solution)/shard_map/jit(dynamic_index_in_dim)/dynamic_slice | solution.py:27
  220.0 11.4 %copy.12 = bf16[32,1,512,64]{3,2,0,1:T(8,128)(2,1)} copy(bf16[32,1,512,64]{2,1,0,3:T(2,128)(2,1)} %constant_dynamic-slice_fusion) | data formatting | bytes 4194304
  231.4 1.1 constant_dynamic-slice_fusion.1
  233.1 1.2 broadcast_in_dim.34
  234.3 56.9 %while.11 = (s32[]{:T(128)}, f32[32,128,64]{1,0,2:T(8,128)}, s32[]{:T(128)}, s32[1024]{0:T(1024)}, bf16[32,128,64]{2,1,0:T(8,128)(2,1)S(1)}, /*index=5*/s32[1024...) while((s32[]{:T(128)}, f32[32,128,64]{1,0,2:T(8,128)}, ...), condition=%wide.region_1.3_spmd.clone, body=%wide.region_0.2_spmd.clone.sunk | while | flops 613769984 | bytes 25313476 | solution.py:68
  235.1 3.1 gather_fusion.2
  238.1 5.2 %gather_fusion.1 = bf16[128,128,64]{2,1,0:T(8,128)(2,1)} fusion(bf16[128,128,64]{2,1,0:T(8,128)(2,1)} %get-tuple-element.230, s32[1024]{0:T(1024)S(1)} %pad_clamp_fusion.4), kind=kCustom, calls=%fused_computation.clone.clone.1 | custom fusion | bytes 4194816 | tf_op jit(solution)/shard_map/while/body/jit(_take)/gather | solution.py:54
  243.4 5.2 %gather_fusion = bf16[128,128,64]{2,1,0:T(8,128)(2,1)} fusion(bf16[128,128,64]{2,1,0:T(8,128)(2,1)} %get-tuple-element.233, s32[1024]{0:T(1024)S(1)} %pad_clamp_fusion.4), kind=kCustom, calls=%fused_computation.1.clone.clone.1 | custom fusion | bytes 4194816 | tf_op jit(solution)/shard_map/while/body/jit(_take)/gather | solution.py:55
  248.6 1.4 fusion.50
  250.0 9.0 %fusion.51 = bf16[128,128,64]{1,2,0:T(8,128)(2,1)S(1)} fusion(bf16[128,128,64]{2,1,0:T(8,128)(2,1)} %gather_fusion, f32[128,128]{1,0:T(8,128)S(1)} %multiply_exponential_fusion.2, f32[128]{0:T(128)S(1)} %fusion.50, pred[128]{0:T(512)(128)(4,1)S(1)} %get-tuple-element.193, bf16[128,128,64]{2,1,0:T(8,128)(2,1)} %gather_fusion.1, ...), kind=kOutput, calls=%fused_computation.7.clone.1 | convolution fusion | flops 546308096 | bytes 8454912 | tf_op jit(solution)/shard_map/while/body/pij,pjk->pik/dot_general | solution.py:63
  259.1 3.6 fusion.52
  263.5 3.1 gather_fusion.2
  266.6 5.2 %gather_fusion.1 = bf16[128,128,64]{2,1,0:T(8,128)(2,1)} fusion(bf16[128,128,64]{2,1,0:T(8,128)(2,1)} %get-tuple-element.230, s32[1024]{0:T(1024)S(1)} %pad_clamp_fusion.4), kind=kCustom, calls=%fused_computation.clone.clone.1 | custom fusion | bytes 4194816 | tf_op jit(solution)/shard_map/while/body/jit(_take)/gather | solution.py:54
  271.8 5.2 %gather_fusion = bf16[128,128,64]{2,1,0:T(8,128)(2,1)} fusion(bf16[128,128,64]{2,1,0:T(8,128)(2,1)} %get-tuple-element.233, s32[1024]{0:T(1024)S(1)} %pad_clamp_fusion.4), kind=kCustom, calls=%fused_computation.1.clone.clone.1 | custom fusion | bytes 4194816 | tf_op jit(solution)/shard_map/while/body/jit(_take)/gather | solution.py:55
  277.0 1.4 fusion.50
  278.5 9.0 %fusion.51 = bf16[128,128,64]{1,2,0:T(8,128)(2,1)S(1)} fusion(bf16[128,128,64]{2,1,0:T(8,128)(2,1)} %gather_fusion, f32[128,128]{1,0:T(8,128)S(1)} %multiply_exponential_fusion.2, f32[128]{0:T(128)S(1)} %fusion.50, pred[128]{0:T(512)(128)(4,1)S(1)} %get-tuple-element.193, bf16[128,128,64]{2,1,0:T(8,128)(2,1)} %gather_fusion.1, ...), kind=kOutput, calls=%fused_computation.7.clone.1 | convolution fusion | flops 546308096 | bytes 8454912 | tf_op jit(solution)/shard_map/while/body/pij,pjk->pik/dot_general | solution.py:63
  287.5 3.6 fusion.52
  291.2 2.8 copy.20
  294.0 200.9 %reduce-scatter.2.cloned.1.call-done = f32[512,64]{0,1:T(8,128)} async-done(((f32[4096,64]{0,1:T(8,128)}), f32[512,64]{0,1:T(8,128)}) %reduce-scatter.2.cloned.1.call-update) | async-done | bytes 131088 | tf_op jit(solution)/shard_map/reduce_scatter | solution.py:70
  (18 shorter events, 3.8 us)
Async XLA Ops:
  6.5 57.3 %all-gather.5.cloned.1.call-start = ((), (), s32[]{:S(2)}) async-start(), calls=%async_computation.2 | async-start | bytes 2162688 | tf_op jit(solution)/shard_map/all_gather | solution.py:23
  7.3 189.7 %all-gather.3.cloned.1.call-start = ((), (), s32[]{:S(2)}) async-start(), calls=%async_computation.1 | async-start | bytes 16842752 | tf_op jit(solution)/shard_map/all_gather | solution.py:22
  8.0 486.9 %reduce-scatter.2.cloned.1.call-start = ((), (), s32[]{:S(2)}) async-start(), calls=%async_computation.3 | async-start | bytes 1179648 | tf_op jit(solution)/shard_map/reduce_scatter | solution.py:70
  209.0 5.7 %copy-start = (bf16[8,8,256,512]{3,2,1,0:T(8,128)(2,1)}, bf16[8,8,256,512]{3,2,1,0:T(8,128)(2,1)S(1)}, u32[]{:S(2)}) copy-start(bf16[8,8,256,512]{3,2,1,0:T(8,128)(2,1)S(1)} %copy.13) | copy-start | bytes 50331652
Sparse Core Ops, SparseCore 0:
  9.8 53.9 all-gather.4
  67.6 129.2 all-gather.2
  294.1 200.7 reduce-scatter.1
where the time goes:
time: 508 us; the launch traced here: 501 us
  waiting for transfers between devices  386 us (76%)
  local copies, waits for them, and re-layouts  71.9 us (14%)
  matrix products  25.3 us (5%)
  between operations  13.8 us (3%)
    reduce_scatter x1, waiting for transfers between devices, local(): lax.psum_scatter(partial_rows, 'cols', scatter_dimension=0, tiled=True)  201 us
    all_gather x1, waiting for transfers between devices, local(): everything = lax.all_gather(anomalies, ('rows', 'cols'), axis=0, tiled=True)  128 us
    all_gather x1, waiting for transfers between devices, local(): col_innov = lax.all_gather(innovations, 'rows', axis=0, tiled=True)  55.1 us
    unnamed x6, local copies, waits for them, and re-layouts  32.5 us
    dot_general x2, matrix products, one_group(): jnp.einsum('pij,pjk->pik', tapered, innov, preferred_element_type=jnp.flo...  18.1 us
    gather x2, local copies, waits for them, and re-layouts, one_group(): right = jnp.take(col_blocks, col_local, axis=0)  10.5 us
    gather x2, local copies, waits for them, and re-layouts, one_group(): innov = jnp.take(innov_blocks, col_local, axis=0)  10.4 us
  transfers between devices with their start and end apart: 3, of which 3 were waited for; matrix products, arithmetic and copies ran while one was open for 1% of the time, Pallas kernels for 0%

commit v1 on v0

v1 whole, which is shorter than its diff:
```python
import functools
import math

import jax
import jax.numpy as jnp
from jax import lax
from jax.experimental import pallas as pl
from jax.experimental.pallas import tpu as pltpu
from jax.sharding import PartitionSpec as P

BLK = 128
SLOTS = 32
TAPER_CELLS = 8
DIST_SCALE = 4.0
DISTS = 8
NY, NX, NZ = 4, 4, 8
MESH = pl.DeviceIdType.MESH
F32, BF16 = jnp.float32, jnp.bfloat16


def slot_lists(rows, cols, dist, count, col_blocks):
    slots = rows.shape[1]
    chunks = range(slots // BLK)
    live = lax.broadcasted_iota(jnp.int32, (1, slots), 1) < count
    held = jnp.where(live, rows, 2 * slots)
    entry = (dist + 1) * col_blocks + cols
    lane = lax.broadcasted_iota(jnp.int32, (BLK, BLK), 1)
    earlier = lax.broadcasted_iota(jnp.int32, (BLK, BLK), 0) < lane

    def part(v, c):
        return v[:, c * BLK : (c + 1) * BLK]

    def down(v, c):
        return jnp.broadcast_to(part(v, c), (BLK, BLK)).T

    held_down = [down(held, c) for c in chunks]
    places = []
    for c in chunks:
        same = jnp.where((held_down[c] == part(held, c)) & earlier, 1, 0)
        for e in range(c):
            same = same + jnp.where(held_down[e] == part(held, c), 1, 0)
        places.append(part(held, c) * SLOTS + jnp.sum(same, axis=0, keepdims=True))
    place = jnp.concatenate(places, axis=1)
    place_down = [down(place, c) for c in chunks]
    entry_down = [down(entry, c) for c in chunks]
    out = []
    for c in chunks:
        found = jnp.zeros((BLK, BLK), jnp.int32)
        for e in chunks:
            found = found + jnp.where(place_down[e] == lane + c * BLK, entry_down[e], 0)
        out.append(jnp.sum(found, axis=0, keepdims=True))
    return jnp.concatenate(out, axis=1)


def kernel(
    count_ref, x_ref, v_ref, rows_ref, cols_ref, dist_ref, out_ref,
    col, row, taper, lists, list_smem, part, own, landed,
    send_sem, recv_sem, rs_send, rs_recv, local_sem,
):
    r, z = lax.axis_index("rows"), lax.axis_index("cols")
    core = lax.rem(r, 2)
    chip = r // 2
    x, y = lax.rem(chip, NX), chip // NX
    members, cells = x_ref.shape
    half = cells // BLK // 2

    def dev(yy, xx):
        return (lax.rem(yy + NY, NY) * NX + lax.rem(xx + NX, NX)) * 2 + core

    def slab(dy, dx, s):
        return (lax.rem(y + dy + NY, NY) * NX + lax.rem(x + dx + NX, NX)) * 2 + s

    sib = r + 1 - 2 * core

    group_rows = cells // BLK
    mine = []
    for n, (src, dst) in enumerate(((x_ref, col.at[0, r]), (v_ref, col.at[1, r]), (x_ref, row.at[z]))):
        for b in range(group_rows):
            mine.append(
                pltpu.make_async_copy(
                    src.at[:, b * BLK : (b + 1) * BLK], dst.at[b], local_sem.at[n * group_rows + b]
                )
            )
    for c in mine:
        c.start()

    barrier = pltpu.get_barrier_semaphore()
    peers = [(sib, z), (dev(y, x + 1), z), (dev(y, x - 1), z), (dev(y + 1, x), z), (dev(y - 1, x), z)]
    peers += [(r, lax.rem(z + k, NZ)) for k in range(1, NZ)]
    for peer in peers:
        pl.semaphore_signal(barrier, inc=1, device_id=peer, device_id_type=MESH)
    for c in mine:
        c.wait()
    pl.semaphore_wait(barrier, len(peers))

    started = []

    def push(src, device, k):
        c = pltpu.make_async_remote_copy(
            src_ref=src, dst_ref=src, send_sem=send_sem.at[k], recv_sem=recv_sem.at[k],
            device_id=device, device_id_type=MESH,
        )
        c.start()
        started.append(c)
        return c

    counter = iter(range(1000))

    def key():
        return next(counter)

    class Kind:
        def __init__(self, other):
            self.s = 1 - core if other else core
            self.fy = self.s
            self.fx = 1 - self.s

        def first(self, d):
            return (dev(y + d * self.fy, x + d * self.fx), z)

        def second(self, d):
            return (dev(y + d * self.fx, x + d * self.fy), z)

        def at(self, o, e):
            return slab(o * self.fy + e * self.fx, o * self.fx + e * self.fy, self.s)

    kinds = [Kind(False), Kind(True)]

    def full(k, o, e):
        return col.at[core, k.at(o, e)]

    def halved(k, o, e, h):
        return col.at[core, k.at(o, e), pl.ds(h * half, half)]

    sib_copies = []

    def to_sib(k, o, e):
        sib_copies.append(push(full(k, o, e), (sib, z), key()))

    ev = {}
    swap = push(col.at[1 - core, r], (sib, z), key())
    own_kind, other_kind = kinds

    def begin(i):
        k = kinds[i]
        for d in (1, -1):
            ev[i, "f", d] = push(full(k, 0, 0), k.first(d), key())
        for d in (1, -1):
            ev[i, "s", 0, d] = push(full(k, 0, 0), k.second(d), key())

    begin(0)
    zev = {}
    zev[1, 1] = push(row.at[z], (r, lax.rem(z + 1, NZ)), key())
    zev[1, -1] = push(row.at[z], (r, lax.rem(z + NZ - 1, NZ)), key())
    to_sib(own_kind, 0, 0)
    swap.wait_recv()
    begin(1)

    i = lax.broadcasted_iota(jnp.int32, (BLK, BLK), 0)
    j = lax.broadcasted_iota(jnp.int32, (BLK, BLK), 1)
    base = jnp.exp(-jnp.abs(i - j).astype(F32) / TAPER_CELLS) * (1.0 / (members - 1))
    taper[0] = jnp.zeros((BLK, BLK), F32)
    for d in range(DISTS):
        taper[d + 1] = base * math.exp(-d / DIST_SCALE)
    col_blocks = col.shape[1] * group_rows
    lists[...] = slot_lists(rows_ref[...], cols_ref[...], dist_ref[...], count_ref[0, 0], col_blocks)
    to_smem = pltpu.make_async_copy(lists, list_smem, local_sem.at[3 * group_rows])
    to_smem.start()

    def zrelay(step):
        for d in (1, -1):
            zev[step, d].wait_recv()
            where = lax.rem(z - d * step + NZ, NZ)
            target = (r, lax.rem(z + d + NZ, NZ))
            if step + 1 < NZ // 2:
                zev[step + 1, d] = push(row.at[where], target, key())
            elif step + 1 == NZ // 2:
                h = 0 if d == 1 else 1
                zev[step + 1, d] = push(row.at[where, pl.ds(h * half, half)], target, key())

    for n, k in enumerate(kinds):
        for d in (1, -1):
            ev[n, "f", d].wait_recv()
            h = 0 if d == 1 else 1
            ev[n, "ff", d] = push(halved(k, -d, 0, h), k.first(d), key())
            for e in (1, -1):
                ev[n, "s", -d, e] = push(full(k, -d, 0), k.second(e), key())
            to_sib(k, -d, 0)
    zrelay(1)
    for n, k in enumerate(kinds):
        for e in (1, -1):
            ev[n, "s", 0, e].wait_recv()
            h = 0 if e == 1 else 1
            ev[n, "sf", 0, e] = push(halved(k, 0, -e, h), k.second(e), key())
            to_sib(k, 0, -e)
    for n, k in enumerate(kinds):
        ev[n, "ff", 1].wait_recv()
        ev[n, "ff", -1].wait_recv()
        for e in (1, -1):
            ev[n, "s", 2, e] = push(full(k, 2, 0), k.second(e), key())
        to_sib(k, 2, 0)
    zrelay(2)
    for o in (-1, 1, 2):
        for n, k in enumerate(kinds):
            for e in (1, -1):
                ev[n, "s", o, e].wait_recv()
                h = 0 if e == 1 else 1
                ev[n, "sf", o, e] = push(halved(k, o, -e, h), k.second(e), key())
                to_sib(k, o, -e)
        if o == -1:
            zrelay(3)
    for o in (0, -1, 1, 2):
        for n, k in enumerate(kinds):
            for e in (1, -1):
                ev[n, "sf", o, e].wait_recv()
            to_sib(k, o, 2)
    for d in (1, -1):
        zev[NZ // 2, d].wait_recv()
    to_smem.wait()
    for c in sib_copies:
        c.wait_recv()

    nt = (((1,), (1,)), ((), ()))

    def entry(a, s):
        e = list_smem[0, a * SLOTS + s]
        q = e & (col_blocks - 1)
        return e // col_blocks, q // group_rows, q & (group_rows - 1)

    def one_block(a, xa):
        total = None
        for s in range(0, SLOTS, 2):
            d0, q0, b0 = entry(a, s)
            d1, q1, b1 = entry(a, s + 1)
            xb = jnp.concatenate([col[0, q0, b0], col[0, q1, b1]], axis=1)
            prod = jnp.dot(xa, xb, preferred_element_type=F32)
            kd = jnp.concatenate([taper[d0], taper[d1]], axis=1)
            t = (prod * kd).astype(BF16)
            vb = jnp.concatenate([col[1, q0, b0], col[1, q1, b1]], axis=1)
            term = lax.dot_general(t, vb, nt, preferred_element_type=F32)
            total = term if total is None else total + term
        return total

    @pl.loop(0, NZ)
    def _(t):
        off = NZ // 2 + (t + 1) // 2 * (1 - 2 * lax.rem(t, 2))
        g = lax.rem(z + off, NZ)

        @pl.loop(0, group_rows)
        def _(b):
            xa = row[g, b].astype(F32).T.astype(BF16)
            y_t = one_block(g * group_rows + b, xa).T
            own[b] = y_t
            part[t, b] = y_t.astype(BF16)

        @pl.when(t < NZ - 1)
        def _():
            pltpu.make_async_remote_copy(
                src_ref=part.at[t], dst_ref=landed.at[t], send_sem=rs_send.at[t], recv_sem=rs_recv.at[t],
                device_id=(r, g), device_id_type=MESH,
            ).start()

    total = own[...]
    for t in range(NZ - 1):
        done = pltpu.make_async_remote_copy(
            src_ref=part.at[t], dst_ref=landed.at[t], send_sem=rs_send.at[t], recv_sem=rs_recv.at[t],
            device_id=(r, lax.rem(z + 1, NZ)), device_id_type=MESH,
        )
        done.wait()
        total = total + landed[t].astype(F32)
    for b in range(group_rows):
        out_ref[:, b * BLK : (b + 1) * BLK] = total[b]
    for c in started:
        c.wait_send()


def local(anomalies, innovations, pair_rows, pair_cols, pair_dist, pair_counts):
    cells, members = anomalies.shape
    columns = innovations.shape[1]
    n_rows = lax.axis_size("rows")
    vm = pl.BlockSpec(memory_space=pltpu.VMEM)
    hbm = pl.BlockSpec(memory_space=pl.ANY)
    each = cells // BLK
    blocks = NZ * each
    out = pl.pallas_call(
        kernel,
        out_shape=jax.ShapeDtypeStruct((columns, cells), F32),
        in_specs=[pl.BlockSpec(memory_space=pltpu.SMEM), hbm, hbm, vm, vm, vm],
        out_specs=vm,
        scratch_shapes=[
            pltpu.VMEM((2, n_rows, each, members, BLK), BF16),
            pltpu.VMEM((NZ, each, members, BLK), BF16),
            pltpu.VMEM((DISTS + 1, BLK, BLK), F32),
            pltpu.VMEM((1, blocks * SLOTS), jnp.int32),
            pltpu.SMEM((1, blocks * SLOTS), jnp.int32),
            pltpu.VMEM((NZ, each, columns, BLK), BF16),
            pltpu.VMEM((each, columns, BLK), F32),
            pltpu.VMEM((NZ - 1, each, columns, BLK), BF16),
            pltpu.SemaphoreType.DMA((96,)),
            pltpu.SemaphoreType.DMA((96,)),
            pltpu.SemaphoreType.DMA((NZ - 1,)),
            pltpu.SemaphoreType.DMA((NZ - 1,)),
            pltpu.SemaphoreType.DMA((3 * each + 1,)),
        ],
        compiler_params=pltpu.CompilerParams(
            collective_id=0, has_side_effects=True, vmem_limit_bytes=48 << 20
        ),
        name="increment",
    )(pair_counts, anomalies.T, innovations.T, pair_rows, pair_cols, pair_dist)
    return out.T


def solution(mesh):
    split = P(("rows", "cols"), None)
    pairs = P("rows", "cols")
    return jax.shard_map(
        local, mesh=mesh, in_specs=(split, split, pairs, pairs, pairs, pairs), out_specs=split, check_vma=False
    )
```

time: 508 us -> 68.6 us (0.14); the launches traced: 501 us -> 68.4 us
  waiting for transfers between devices: 386 us -> 0 us
  local copies, waits for them, and re-layouts: 71.9 us -> 3.73 us
  Pallas kernels: 0 us -> 64 us
  matrix products: 25.3 us -> 0 us
  between operations: 13.8 us -> 0.68 us
    reduce_scatter x1 -> x0, waiting for transfers between devices: 201 us -> none  [local(): lax.psum_scatter(partial_rows, 'cols', scatter_dimension=0, tiled=True)]
    all_gather x2 -> x0, waiting for transfers between devices: 183 us -> none  [the longest x1 128 us: local(): everything = lax.all_gather(anomalies, ('rows', 'cols'), axis=0, tiled=True)]
    pallas_call x0 -> x1, Pallas kernels: none -> 64 us  [local(): pl.pallas_call(kernel, out_shape=jax.ShapeDtypeStruct((columns, cells), F...]
    unnamed x6 -> x11, local copies, waits for them, and re-layouts: 32.5 us -> 3.73 us
    gather x6 -> x0, local copies, waits for them, and re-layouts: 27 us -> none  [the longest x2 10.5 us: one_group(): right = jnp.take(col_blocks, col_local, axis=0)]
    dot_general x4 -> x0, matrix products: 25.3 us -> none  [the longest x2 18.1 us: one_group(): jnp.einsum('pij,pjk->pik', tapered, innov, preferred_element_type=jnp.flo...]
    dynamic_slice x2 -> x0, local copies, waits for them, and re-layouts: 6.36 us -> none  [the longest x1 5.28 us: local(): lax.dynamic_index_in_dim(all_cells, lax.axis_index('cols'), 1, keepdims=F...]
  transfers between devices with their start and end apart: 3 -> 0, of which waited for: 3 -> 0; matrix products, arithmetic and copies ran while one was open for 1% -> 0% of each run, Pallas kernels for 0% -> 0%
where the time goes in v1:
time: 68.6 us; the launch traced here: 68.4 us
  Pallas kernels  64 us (93%)
  local copies, waits for them, and re-layouts  3.73 us (5%)
    pallas_call x1, Pallas kernels, local(): pl.pallas_call(kernel, out_shape=jax.ShapeDtypeStruct((columns, cells), F...  64 us
    unnamed x11, local copies, waits for them, and re-layouts  3.73 us

profile of v1, /device:TPU:1, one launch (start us, length us, event | category | flops | bytes accessed | tf_op | source)
XLA Modules:
  0.0 68.4 jit_solution(11622762898717597412)
XLA Ops:
  0.0 0.0 copy-start.2
  0.7 0.0 copy-done.2
  0.7 0.0 copy-start
  0.7 0.8 %copy-done = bf16[512,64]{0,1:T(8,128)(2,1)S(1)} copy-done((bf16[512,64]{0,1:T(8,128)(2,1)S(1)}, bf16[512,64]{0,1:T(8,128)(2,1)}, u32[]{:S(2)}) %copy-start) | copy-done | bytes 65560
  1.5 0.0 copy-start.1
  1.5 0.8 %copy-done.1 = bf16[512,64]{0,1:T(8,128)(2,1)S(1)} copy-done((bf16[512,64]{0,1:T(8,128)(2,1)S(1)}, bf16[512,64]{0,1:T(8,128)(2,1)}, u32[]{:S(2)}) %copy-start.1) | copy-done | bytes 65560
  2.4 0.0 copy-start.3
  2.4 0.7 %copy-done.3 = s32[1,1024]{1,0:T(1,128)S(1)} copy-done((s32[1,1024]{1,0:T(1,128)S(1)}, s32[1,1024]{1,0:T(1,128)}, u32[]{:S(2)}) %copy-start.3) | copy-done | bytes 4120
  3.1 0.0 copy-start.4
  3.1 0.7 %copy-done.4 = s32[1,1024]{1,0:T(1,128)S(1)} copy-done((s32[1,1024]{1,0:T(1,128)S(1)}, s32[1,1024]{1,0:T(1,128)}, u32[]{:S(2)}) %copy-start.4) | copy-done | bytes 4120
  3.7 64.0 %increment.1 = f32[64,512]{1,0:T(8,128)S(1)} custom-call(s32[1,1]{1,0:T(1,128)S(6)} %copy.8.count_ref, bf16[64,512]{1,0:T(8,128)(2,1)S(1)} %bitcast.4, bf16[64,512]{1,0:T(8,128)(2,1)S(1)} %bitcast.5, s32[1,1024]{1,0:T(1,128)S(1)} %copy-done.2, s32[1,1024]{1,0:T(1,128)S(1)} %copy-done.3, s32[1,1024]{1,0:T(1,128)S(1)} %copy-done.4), custom_call_target="tpu_custom_call" | custom-call | tf_op jit(solution)/shard_map/increment/pallas_call | solution.py:285
  67.7 0.7 copy.9
Async XLA Ops:
  0.0 0.7 %copy-start.2 = (s32[1,1024]{1,0:T(1,128)S(1)}, s32[1,1024]{1,0:T(1,128)}, u32[]{:S(2)}) copy-start(s32[1,1024]{1,0:T(1,128)} %rows_ref.1) | copy-start | bytes 12292
  0.7 0.8 %copy-start = (bf16[512,64]{0,1:T(8,128)(2,1)S(1)}, bf16[512,64]{0,1:T(8,128)(2,1)}, u32[]{:S(2)}) copy-start(bf16[512,64]{0,1:T(8,128)(2,1)} %param.6) | copy-start | bytes 196612
  1.5 0.8 %copy-start.1 = (bf16[512,64]{0,1:T(8,128)(2,1)S(1)}, bf16[512,64]{0,1:T(8,128)(2,1)}, u32[]{:S(2)}) copy-start(bf16[512,64]{0,1:T(8,128)(2,1)} %param.7) | copy-start | bytes 196612
  2.4 0.7 %copy-start.3 = (s32[1,1024]{1,0:T(1,128)S(1)}, s32[1,1024]{1,0:T(1,128)}, u32[]{:S(2)}) copy-start(s32[1,1024]{1,0:T(1,128)} %cols_ref.1) | copy-start | bytes 12292
  3.1 0.7 %copy-start.4 = (s32[1,1024]{1,0:T(1,128)S(1)}, s32[1,1024]{1,0:T(1,128)}, u32[]{:S(2)}) copy-start(s32[1,1024]{1,0:T(1,128)} %dist_ref.1) | copy-start | bytes 12292

commit v2 on v1

--- a/solution.py
+++ b/solution.py
@@ -10,6 +10,7 @@
 
 BLK = 128
 SLOTS = 32
+GROUP = 8
 TAPER_CELLS = 8
 DIST_SCALE = 4.0
 DISTS = 8
@@ -54,7 +55,7 @@
 
 def kernel(
     count_ref, x_ref, v_ref, rows_ref, cols_ref, dist_ref, out_ref,
-    col, row, taper, lists, list_smem, part, own, landed,
+    count, pairs, col, row, taper, lists, list_smem, part, own, landed,
     send_sem, recv_sem, rs_send, rs_recv, local_sem,
 ):
     r, z = lax.axis_index("rows"), lax.axis_index("cols")
@@ -83,6 +84,11 @@
             )
     for c in mine:
         c.start()
+    listed = [pltpu.make_async_copy(count_ref, count, local_sem.at[3 * group_rows])]
+    for n, ref in enumerate((rows_ref, cols_ref, dist_ref)):
+        listed.append(pltpu.make_async_copy(ref, pairs.at[n], local_sem.at[3 * group_rows + 1 + n]))
+    for c in listed:
+        c.start()
 
     barrier = pltpu.get_barrier_semaphore()
     peers = [(sib, z), (dev(y, x + 1), z), (dev(y, x - 1), z), (dev(y + 1, x), z), (dev(y - 1, x), z)]
@@ -163,8 +169,10 @@
     for d in range(DISTS):
         taper[d + 1] = base * math.exp(-d / DIST_SCALE)
     col_blocks = col.shape[1] * group_rows
-    lists[...] = slot_lists(rows_ref[...], cols_ref[...], dist_ref[...], count_ref[0, 0], col_blocks)
-    to_smem = pltpu.make_async_copy(lists, list_smem, local_sem.at[3 * group_rows])
+    for c in listed:
+        c.wait()
+    lists[...] = slot_lists(pairs[0], pairs[1], pairs[2], count[0, 0], col_blocks)
+    to_smem = pltpu.make_async_copy(lists, list_smem, local_sem.at[3 * group_rows + 4])
     to_smem.start()
 
     def zrelay(step):
@@ -220,38 +228,43 @@
     for c in sib_copies:
         c.wait_recv()
 
-    nt = (((1,), (1,)), ((), ()))
+    tn = (((0,), (0,)), ((), ()))
 
     def entry(a, s):
         e = list_smem[0, a * SLOTS + s]
         q = e & (col_blocks - 1)
         return e // col_blocks, q // group_rows, q & (group_rows - 1)
 
-    def one_block(a, xa):
-        total = None
-        for s in range(0, SLOTS, 2):
-            d0, q0, b0 = entry(a, s)
-            d1, q1, b1 = entry(a, s + 1)
-            xb = jnp.concatenate([col[0, q0, b0], col[0, q1, b1]], axis=1)
-            prod = jnp.dot(xa, xb, preferred_element_type=F32)
-            kd = jnp.concatenate([taper[d0], taper[d1]], axis=1)
-            t = (prod * kd).astype(BF16)
-            vb = jnp.concatenate([col[1, q0, b0], col[1, q1, b1]], axis=1)
-            term = lax.dot_general(t, vb, nt, preferred_element_type=F32)
-            total = term if total is None else total + term
-        return total
-
     @pl.loop(0, NZ)
     def _(t):
         off = NZ // 2 + (t + 1) // 2 * (1 - 2 * lax.rem(t, 2))
         g = lax.rem(z + off, NZ)
-
-        @pl.loop(0, group_rows)
-        def _(b):
-            xa = row[g, b].astype(F32).T.astype(BF16)
-            y_t = one_block(g * group_rows + b, xa).T
-            own[b] = y_t
-            part[t, b] = y_t.astype(BF16)
+        turns = SLOTS // GROUP
+        steps = turns * group_rows
+        products, tapered, sums = {}, {}, {}
+        for i in range(steps + 2):
+            if i < steps:
+                b = i // turns
+                xa = row[g, b]
+                entries = [entry(g * group_rows + b, i % turns * GROUP + n) for n in range(GROUP)]
+                products[i] = entries, [
+                    lax.dot_general(col[0, q, k], xa, tn, preferred_element_type=F32) for _, q, k in entries
+                ]
+            if 1 <= i <= steps:
+                entries, prods = products.pop(i - 1)
+                tapered[i - 1] = entries, jnp.concatenate(
+                    [(p * taper[d]).astype(BF16) for p, (d, _, _) in zip(prods, entries)], axis=0
+                )
+            if i >= 2:
+                b, turn = divmod(i - 2, turns)
+                entries, weights = tapered.pop(i - 2)
+                vb = jnp.concatenate([col[1, q, k] for _, q, k in entries], axis=1)
+                term = jnp.dot(vb, weights, preferred_element_type=F32)
+                sums[b] = term if turn == 0 else sums[b] + term
+                if turn == turns - 1:
+                    done = sums.pop(b)
+                    own[b] = done
+                    part[t, b] = done.astype(BF16)
 
         @pl.when(t < NZ - 1)
         def _():
@@ -279,15 +292,17 @@
     columns = innovations.shape[1]
     n_rows = lax.axis_size("rows")
     vm = pl.BlockSpec(memory_space=pltpu.VMEM)
-    hbm = pl.BlockSpec(memory_space=pl.ANY)
+    hbm = pl.BlockSpec(memory_space=pltpu.HBM)
     each = cells // BLK
     blocks = NZ * each
     out = pl.pallas_call(
         kernel,
         out_shape=jax.ShapeDtypeStruct((columns, cells), F32),
-        in_specs=[pl.BlockSpec(memory_space=pltpu.SMEM), hbm, hbm, vm, vm, vm],
+        in_specs=[hbm] * 6,
         out_specs=vm,
         scratch_shapes=[
+            pltpu.SMEM(pair_counts.shape, jnp.int32),
+            pltpu.VMEM((3,) + pair_rows.shape, jnp.int32),
             pltpu.VMEM((2, n_rows, each, members, BLK), BF16),
             pltpu.VMEM((NZ, each, members, BLK), BF16),
             pltpu.VMEM((DISTS + 1, BLK, BLK), F32),
@@ -300,7 +315,7 @@
             pltpu.SemaphoreType.DMA((96,)),
             pltpu.SemaphoreType.DMA((NZ - 1,)),
             pltpu.SemaphoreType.DMA((NZ - 1,)),
-            pltpu.SemaphoreType.DMA((3 * each + 1,)),
+            pltpu.SemaphoreType.DMA((3 * each + 5,)),
         ],
         compiler_params=pltpu.CompilerParams(
             collective_id=0, has_side_effects=True, vmem_limit_bytes=48 << 20

time: 68.6 us -> 54.6 us (0.80)
  Pallas kernels: 64 us -> 50 us
    pallas_call x1, Pallas kernels: 64 us -> 50 us  [local(): pl.pallas_call(kernel, out_shape=jax.ShapeDtypeStruct((columns, cells), F...]
where the time goes in v2:
time: 54.6 us; the launch traced here: 54.4 us
  Pallas kernels  50 us (92%)
  local copies, waits for them, and re-layouts  3.73 us (7%)
  between operations  0.68 us (1%)
    pallas_call x1, Pallas kernels, local(): pl.pallas_call(kernel, out_shape=jax.ShapeDtypeStruct((columns, cells), F...  50 us
    unnamed x11, local copies, waits for them, and re-layouts  3.73 us

profile of v2, /device:TPU:1, one launch (start us, length us, event | category | flops | bytes accessed | tf_op | source)
XLA Modules:
  0.0 54.4 jit_solution(5406065707444292077)
XLA Ops:
  0.0 0.0 copy-start.2
  0.7 0.0 copy-done.2
  0.7 0.0 copy-start
  0.7 0.8 %copy-done = bf16[512,64]{0,1:T(8,128)(2,1)S(1)} copy-done((bf16[512,64]{0,1:T(8,128)(2,1)S(1)}, bf16[512,64]{0,1:T(8,128)(2,1)}, u32[]{:S(2)}) %copy-start) | copy-done | bytes 65560
  1.5 0.0 copy-start.1
  1.5 0.8 %copy-done.1 = bf16[512,64]{0,1:T(8,128)(2,1)S(1)} copy-done((bf16[512,64]{0,1:T(8,128)(2,1)S(1)}, bf16[512,64]{0,1:T(8,128)(2,1)}, u32[]{:S(2)}) %copy-start.1) | copy-done | bytes 65560
  2.4 0.0 copy-start.3
  2.4 0.7 %copy-done.3 = s32[1,1024]{1,0:T(1,128)S(1)} copy-done((s32[1,1024]{1,0:T(1,128)S(1)}, s32[1,1024]{1,0:T(1,128)}, u32[]{:S(2)}) %copy-start.3) | copy-done | bytes 4120
  3.1 0.0 copy-start.4
  3.1 0.7 %copy-done.4 = s32[1,1024]{1,0:T(1,128)S(1)} copy-done((s32[1,1024]{1,0:T(1,128)S(1)}, s32[1,1024]{1,0:T(1,128)}, u32[]{:S(2)}) %copy-start.4) | copy-done | bytes 4120
  3.7 50.0 %increment.1 = f32[64,512]{1,0:T(8,128)S(1)} custom-call(s32[1,1]{1,0:T(1,128)S(6)} %copy.8.count_ref, bf16[64,512]{1,0:T(8,128)(2,1)S(1)} %bitcast.4, bf16[64,512]{1,0:T(8,128)(2,1)S(1)} %bitcast.5, s32[1,1024]{1,0:T(1,128)S(1)} %copy-done.2, s32[1,1024]{1,0:T(1,128)S(1)} %copy-done.3, s32[1,1024]{1,0:T(1,128)S(1)} %copy-done.4), custom_call_target="tpu_custom_call" | custom-call | tf_op jit(solution)/shard_map/increment/pallas_call | solution.py:298
  53.7 0.7 %copy.9 = f32[512,64]{0,1:T(8,128)} copy(f32[512,64]{0,1:T(8,128)S(1)} %bitcast.3) | data formatting | bytes 262144
Async XLA Ops:
  0.0 0.7 %copy-start.2 = (s32[1,1024]{1,0:T(1,128)S(1)}, s32[1,1024]{1,0:T(1,128)}, u32[]{:S(2)}) copy-start(s32[1,1024]{1,0:T(1,128)} %rows_ref.1) | copy-start | bytes 12292
  0.7 0.8 %copy-start = (bf16[512,64]{0,1:T(8,128)(2,1)S(1)}, bf16[512,64]{0,1:T(8,128)(2,1)}, u32[]{:S(2)}) copy-start(bf16[512,64]{0,1:T(8,128)(2,1)} %param.6) | copy-start | bytes 196612
  1.5 0.8 %copy-start.1 = (bf16[512,64]{0,1:T(8,128)(2,1)S(1)}, bf16[512,64]{0,1:T(8,128)(2,1)}, u32[]{:S(2)}) copy-start(bf16[512,64]{0,1:T(8,128)(2,1)} %param.7) | copy-start | bytes 196612
  2.4 0.7 %copy-start.3 = (s32[1,1024]{1,0:T(1,128)S(1)}, s32[1,1024]{1,0:T(1,128)}, u32[]{:S(2)}) copy-start(s32[1,1024]{1,0:T(1,128)} %cols_ref.1) | copy-start | bytes 12292
  3.1 0.7 %copy-start.4 = (s32[1,1024]{1,0:T(1,128)S(1)}, s32[1,1024]{1,0:T(1,128)}, u32[]{:S(2)}) copy-start(s32[1,1024]{1,0:T(1,128)} %dist_ref.1) | copy-start | bytes 12292

commit v3 on v2

--- a/solution.py
+++ b/solution.py
@@ -16,6 +16,7 @@
 DISTS = 8
 NY, NX, NZ = 4, 4, 8
 MESH = pl.DeviceIdType.MESH
+RING = (1, -1, 2)
 F32, BF16 = jnp.float32, jnp.bfloat16
 
 
@@ -56,20 +57,16 @@
 def kernel(
     count_ref, x_ref, v_ref, rows_ref, cols_ref, dist_ref, out_ref,
     count, pairs, col, row, taper, lists, list_smem, part, own, landed,
-    send_sem, recv_sem, rs_send, rs_recv, local_sem,
+    send_sem, recv_sem, rs_send, rs_recv, local_sem, ready,
 ):
     r, z = lax.axis_index("rows"), lax.axis_index("cols")
     core = lax.rem(r, 2)
     chip = r // 2
     x, y = lax.rem(chip, NX), chip // NX
     members, cells = x_ref.shape
-    half = cells // BLK // 2
 
     def dev(yy, xx):
         return (lax.rem(yy + NY, NY) * NX + lax.rem(xx + NX, NX)) * 2 + core
-
-    def slab(dy, dx, s):
-        return (lax.rem(y + dy + NY, NY) * NX + lax.rem(x + dx + NX, NX)) * 2 + s
 
     sib = r + 1 - 2 * core
 
@@ -91,76 +88,72 @@
         c.start()
 
     barrier = pltpu.get_barrier_semaphore()
-    peers = [(sib, z), (dev(y, x + 1), z), (dev(y, x - 1), z), (dev(y + 1, x), z), (dev(y - 1, x), z)]
-    peers += [(r, lax.rem(z + k, NZ)) for k in range(1, NZ)]
+    peers = [(sib, z)]
+    peers += [(dev(y, x + d), z) for d in RING] + [(dev(y + d, x), z) for d in RING]
     for peer in peers:
         pl.semaphore_signal(barrier, inc=1, device_id=peer, device_id_type=MESH)
+    for k in range(1, NZ):
+        @pl.when(z + k < NZ)
+        def _():
+            pl.semaphore_signal(barrier, inc=1, device_id=(r, lax.rem(z + k, NZ)), device_id_type=MESH)
+
     for c in mine:
         c.wait()
-    pl.semaphore_wait(barrier, len(peers))
+    pl.semaphore_wait(barrier, len(peers) + z)
+    for k in range(1, NZ):
+        @pl.when(z + k >= NZ)
+        def _():
+            pl.semaphore_signal(ready, inc=1, device_id=(r, lax.rem(z + k, NZ)), device_id_type=MESH)
 
     started = []
 
-    def push(src, device, k):
+    def copy(src, device, k):
         c = pltpu.make_async_remote_copy(
             src_ref=src, dst_ref=src, send_sem=send_sem.at[k], recv_sem=recv_sem.at[k],
             device_id=device, device_id_type=MESH,
         )
-        c.start()
         started.append(c)
         return c
 
+    def push(src, device, k):
+        c = copy(src, device, k)
+        c.start()
+        return c
+
     counter = iter(range(1000))
 
     def key():
         return next(counter)
 
-    class Kind:
-        def __init__(self, other):
-            self.s = 1 - core if other else core
-            self.fy = self.s
-            self.fx = 1 - self.s
-
-        def first(self, d):
-            return (dev(y + d * self.fy, x + d * self.fx), z)
-
-        def second(self, d):
-            return (dev(y + d * self.fx, x + d * self.fy), z)
-
-        def at(self, o, e):
-            return slab(o * self.fy + e * self.fx, o * self.fx + e * self.fy, self.s)
-
-    kinds = [Kind(False), Kind(True)]
-
-    def full(k, o, e):
-        return col.at[core, k.at(o, e)]
-
-    def halved(k, o, e, h):
-        return col.at[core, k.at(o, e), pl.ds(h * half, half)]
-
+    def place(n, o, e):
+        return dev(y + (o if n else e), x + (e if n else o))
+
+    def slab(n, o, e):
+        return col.at[n, place(n, o, e)]
+
+    ev = {}
     sib_copies = []
 
-    def to_sib(k, o, e):
-        sib_copies.append(push(full(k, o, e), (sib, z), key()))
-
-    ev = {}
-    swap = push(col.at[1 - core, r], (sib, z), key())
-    own_kind, other_kind = kinds
-
-    def begin(i):
-        k = kinds[i]
-        for d in (1, -1):
-            ev[i, "f", d] = push(full(k, 0, 0), k.first(d), key())
-        for d in (1, -1):
-            ev[i, "s", 0, d] = push(full(k, 0, 0), k.second(d), key())
-
-    begin(0)
-    zev = {}
-    zev[1, 1] = push(row.at[z], (r, lax.rem(z + 1, NZ)), key())
-    zev[1, -1] = push(row.at[z], (r, lax.rem(z + NZ - 1, NZ)), key())
-    to_sib(own_kind, 0, 0)
-    swap.wait_recv()
-    begin(1)
+    def to_sib(n, o, e):
+        sib_copies.append(push(slab(n, o, e), (sib, z), key()))
+
+    def along_second(n, o):
+        for e in RING:
+            ev[n, o, e] = push(slab(n, o, 0), (place(n, 0, e), z), key())
+
+    for d in RING:
+        for n in range(2):
+            ev[n, d] = push(slab(n, 0, 0), (place(n, d, 0), z), key())
+    for n in range(2):
+        along_second(n, 0)
+    zev = [copy(row.at[z], (r, lax.rem(z + k, NZ)), key()) for k in range(1, NZ)]
+    for k in range(1, NZ):
+        @pl.when(z + k >= NZ)
+        def _():
+            zev[k - 1].start()
+
+    for n in range(2):
+        to_sib(n, 0, 0)
 
     i = lax.broadcasted_iota(jnp.int32, (BLK, BLK), 0)
     j = lax.broadcasted_iota(jnp.int32, (BLK, BLK), 1)
@@ -175,55 +168,27 @@
     to_smem = pltpu.make_async_copy(lists, list_smem, local_sem.at[3 * group_rows + 4])
     to_smem.start()
 
-    def zrelay(step):
-        for d in (1, -1):
-            zev[step, d].wait_recv()
-            where = lax.rem(z - d * step + NZ, NZ)
-            target = (r, lax.rem(z + d + NZ, NZ))
-            if step + 1 < NZ // 2:
-                zev[step + 1, d] = push(row.at[where], target, key())
-            elif step + 1 == NZ // 2:
-                h = 0 if d == 1 else 1
-                zev[step + 1, d] = push(row.at[where, pl.ds(h * half, half)], target, key())
-
-    for n, k in enumerate(kinds):
-        for d in (1, -1):
-            ev[n, "f", d].wait_recv()
-            h = 0 if d == 1 else 1
-            ev[n, "ff", d] = push(halved(k, -d, 0, h), k.first(d), key())
-            for e in (1, -1):
-                ev[n, "s", -d, e] = push(full(k, -d, 0), k.second(e), key())
-            to_sib(k, -d, 0)
-    zrelay(1)
-    for n, k in enumerate(kinds):
-        for e in (1, -1):
-            ev[n, "s", 0, e].wait_recv()
-            h = 0 if e == 1 else 1
-            ev[n, "sf", 0, e] = push(halved(k, 0, -e, h), k.second(e), key())
-            to_sib(k, 0, -e)
-    for n, k in enumerate(kinds):
-        ev[n, "ff", 1].wait_recv()
-        ev[n, "ff", -1].wait_recv()
-        for e in (1, -1):
-            ev[n, "s", 2, e] = push(full(k, 2, 0), k.second(e), key())
-        to_sib(k, 2, 0)
-    zrelay(2)
-    for o in (-1, 1, 2):
-        for n, k in enumerate(kinds):
-            for e in (1, -1):
-                ev[n, "s", o, e].wait_recv()
-                h = 0 if e == 1 else 1
-                ev[n, "sf", o, e] = push(halved(k, o, -e, h), k.second(e), key())
-                to_sib(k, o, -e)
-        if o == -1:
-            zrelay(3)
-    for o in (0, -1, 1, 2):
-        for n, k in enumerate(kinds):
-            for e in (1, -1):
-                ev[n, "sf", o, e].wait_recv()
-            to_sib(k, o, 2)
-    for d in (1, -1):
-        zev[NZ // 2, d].wait_recv()
+    for d in RING:
+        for n in range(2):
+            ev[n, d].wait_recv()
+            along_second(n, -d)
+            to_sib(n, -d, 0)
+    @pl.when(z < NZ - 1)
+    def _():
+        pl.semaphore_wait(ready, NZ - 1 - z)
+
+    for k in range(1, NZ):
+        @pl.when(z + k < NZ)
+        def _():
+            zev[k - 1].start()
+
+    for o in (0,) + RING:
+        for e in RING:
+            for n in range(2):
+                ev[n, -o, e].wait_recv()
+                to_sib(n, -o, -e)
+    for c in zev:
+        c.wait_recv()
     to_smem.wait()
     for c in sib_copies:
         c.wait_recv()
@@ -237,8 +202,7 @@
 
     @pl.loop(0, NZ)
     def _(t):
-        off = NZ // 2 + (t + 1) // 2 * (1 - 2 * lax.rem(t, 2))
-        g = lax.rem(z + off, NZ)
+        g = lax.rem(z + 1 + t, NZ)
         turns = SLOTS // GROUP
         steps = turns * group_rows
         products, tapered, sums = {}, {}, {}
@@ -316,9 +280,10 @@
             pltpu.SemaphoreType.DMA((NZ - 1,)),
             pltpu.SemaphoreType.DMA((NZ - 1,)),
             pltpu.SemaphoreType.DMA((3 * each + 5,)),
+            pltpu.SemaphoreType.REGULAR,
         ],
         compiler_params=pltpu.CompilerParams(
-            collective_id=0, has_side_effects=True, vmem_limit_bytes=48 << 20
+            collective_id=0, has_side_effects=True, vmem_limit_bytes=56 << 20
         ),
         name="increment",
     )(pair_counts, anomalies.T, innovations.T, pair_rows, pair_cols, pair_dist)

time: 54.6 us -> 52.3 us (0.958)
  local copies, waits for them, and re-layouts: 3.73 us -> 1.57 us
    unnamed x11 -> x1, local copies, waits for them, and re-layouts: 3.73 us -> 1.57 us
where the time goes in v3:
time: 52.3 us; the launch traced here: 52.2 us
  Pallas kernels  49.9 us (95%)
  local copies, waits for them, and re-layouts  1.57 us (3%)
  between operations  0.66 us (1%)
    pallas_call x1, Pallas kernels, local(): pl.pallas_call(kernel, out_shape=jax.ShapeDtypeStruct((columns, cells), F...  49.9 us
    unnamed x1, local copies, waits for them, and re-layouts  1.57 us

profile of v3, /device:TPU:1, one launch (start us, length us, event | category | flops | bytes accessed | tf_op | source)
XLA Modules:
  0.0 52.2 jit_solution(1865999013672593677)
XLA Ops:
  0.7 49.9 %increment.1 = f32[64,512]{1,0:T(8,128)} custom-call(s32[1,1]{1,0:T(1,128)S(6)} %copy.8.count_ref, bf16[64,512]{1,0:T(8,128)(2,1)} %bitcast.4, bf16[64,512]{1,0:T(8,128)(2,1)} %bitcast.5, s32[1,1024]{1,0:T(1,128)} %rows_ref.1, s32[1,1024]{1,0:T(1,128)} %cols_ref.1, s32[1,1024]{1,0:T(1,128)} %dist_ref.1), custom_call_target="tpu_custom_call" | custom-call | tf_op jit(solution)/shard_map/increment/pallas_call | solution.py:262
  50.6 1.6 %copy.9 = f32[512,64]{0,1:T(8,128)} copy(f32[512,64]{0,1:T(8,128)} %bitcast.3) | data formatting | bytes 262144

commit v4 on v3

--- a/solution.py
+++ b/solution.py
@@ -200,9 +200,17 @@
         q = e & (col_blocks - 1)
         return e // col_blocks, q // group_rows, q & (group_rows - 1)
 
+    def target(t):
+        half = NZ // 2
+        low = z // half * half
+        sign = 1 - 2 * lax.rem(z, 2)
+        across = (half - low) + lax.rem(z + sign * t + half, half)
+        near = low + lax.rem(z + t + 1, half)
+        return jnp.where(t < half, across, near)
+
     @pl.loop(0, NZ)
     def _(t):
-        g = lax.rem(z + 1 + t, NZ)
+        g = target(t)
         turns = SLOTS // GROUP
         steps = turns * group_rows
         products, tapered, sums = {}, {}, {}
@@ -233,18 +241,19 @@
         @pl.when(t < NZ - 1)
         def _():
             pltpu.make_async_remote_copy(
-                src_ref=part.at[t], dst_ref=landed.at[t], send_sem=rs_send.at[t], recv_sem=rs_recv.at[t],
+                src_ref=part.at[t], dst_ref=landed.at[z], send_sem=rs_send.at[t], recv_sem=rs_recv.at[z],
                 device_id=(r, g), device_id_type=MESH,
             ).start()
 
     total = own[...]
-    for t in range(NZ - 1):
+    for k in range(1, NZ):
+        source = lax.rem(z + k, NZ)
         done = pltpu.make_async_remote_copy(
-            src_ref=part.at[t], dst_ref=landed.at[t], send_sem=rs_send.at[t], recv_sem=rs_recv.at[t],
-            device_id=(r, lax.rem(z + 1, NZ)), device_id_type=MESH,
+            src_ref=part.at[k - 1], dst_ref=landed.at[source], send_sem=rs_send.at[k - 1],
+            recv_sem=rs_recv.at[source], device_id=(r, source), device_id_type=MESH,
         )
         done.wait()
-        total = total + landed[t].astype(F32)
+        total = total + landed[source].astype(F32)
     for b in range(group_rows):
         out_ref[:, b * BLK : (b + 1) * BLK] = total[b]
     for c in started:
@@ -274,11 +283,11 @@
             pltpu.SMEM((1, blocks * SLOTS), jnp.int32),
             pltpu.VMEM((NZ, each, columns, BLK), BF16),
             pltpu.VMEM((each, columns, BLK), F32),
-            pltpu.VMEM((NZ - 1, each, columns, BLK), BF16),
+            pltpu.VMEM((NZ, each, columns, BLK), BF16),
             pltpu.SemaphoreType.DMA((96,)),
             pltpu.SemaphoreType.DMA((96,)),
             pltpu.SemaphoreType.DMA((NZ - 1,)),
-            pltpu.SemaphoreType.DMA((NZ - 1,)),
+            pltpu.SemaphoreType.DMA((NZ,)),
             pltpu.SemaphoreType.DMA((3 * each + 5,)),
             pltpu.SemaphoreType.REGULAR,
         ],

time: 52.3 us -> 50.4 us (0.964)
  Pallas kernels: 49.9 us -> 48 us
    pallas_call x1, Pallas kernels: 49.9 us -> 48 us  [local(): pl.pallas_call(kernel, out_shape=jax.ShapeDtypeStruct((columns, cells), F...]
where the time goes in v4:
time: 50.4 us; the launch traced here: 50.2 us
  Pallas kernels  48 us (95%)
  local copies, waits for them, and re-layouts  1.57 us (3%)
  between operations  0.66 us (1%)
    pallas_call x1, Pallas kernels, local(): pl.pallas_call(kernel, out_shape=jax.ShapeDtypeStruct((columns, cells), F...  48 us
    unnamed x1, local copies, waits for them, and re-layouts  1.57 us

profile of v4, /device:TPU:1, one launch (start us, length us, event | category | flops | bytes accessed | tf_op | source)
XLA Modules:
  0.0 50.2 jit_solution(5799143685996007582)
XLA Ops:
  0.7 48.0 %increment.1 = f32[64,512]{1,0:T(8,128)} custom-call(s32[1,1]{1,0:T(1,128)S(6)} %copy.8.count_ref, bf16[64,512]{1,0:T(8,128)(2,1)} %bitcast.4, bf16[64,512]{1,0:T(8,128)(2,1)} %bitcast.5, s32[1,1024]{1,0:T(1,128)} %rows_ref.1, s32[1,1024]{1,0:T(1,128)} %cols_ref.1, s32[1,1024]{1,0:T(1,128)} %dist_ref.1), custom_call_target="tpu_custom_call" | custom-call | tf_op jit(solution)/shard_map/increment/pallas_call | solution.py:271
  48.7 1.6 %copy.9 = f32[512,64]{0,1:T(8,128)} copy(f32[512,64]{0,1:T(8,128)} %bitcast.3) | data formatting | bytes 262144

commit v5 on v4

--- a/solution.py
+++ b/solution.py
@@ -203,8 +203,7 @@
     def target(t):
         half = NZ // 2
         low = z // half * half
-        sign = 1 - 2 * lax.rem(z, 2)
-        across = (half - low) + lax.rem(z + sign * t + half, half)
+        across = (half - low) + t + lax.rem(z, 2) * (1 - 2 * lax.rem(t, 2))
         near = low + lax.rem(z + t + 1, half)
         return jnp.where(t < half, across, near)
 

time: 50.4 us -> 49.1 us (0.974)
  Pallas kernels: 48 us -> 46.7 us
    pallas_call x1, Pallas kernels: 48 us -> 46.7 us  [local(): pl.pallas_call(kernel, out_shape=jax.ShapeDtypeStruct((columns, cells), F...]
where the time goes in v5:
time: 49.1 us; the launch traced here: 49 us
  Pallas kernels  46.7 us (95%)
  local copies, waits for them, and re-layouts  1.57 us (3%)
  between operations  0.66 us (1%)
    pallas_call x1, Pallas kernels, local(): pl.pallas_call(kernel, out_shape=jax.ShapeDtypeStruct((columns, cells), F...  46.7 us
    unnamed x1, local copies, waits for them, and re-layouts  1.57 us

profile of v5, /device:TPU:1, one launch (start us, length us, event | category | flops | bytes accessed | tf_op | source)
XLA Modules:
  0.0 49.0 jit_solution(70224688899558047)
XLA Ops:
  0.7 46.7 %increment.1 = f32[64,512]{1,0:T(8,128)} custom-call(s32[1,1]{1,0:T(1,128)S(6)} %copy.8.count_ref, bf16[64,512]{1,0:T(8,128)(2,1)} %bitcast.4, bf16[64,512]{1,0:T(8,128)(2,1)} %bitcast.5, s32[1,1024]{1,0:T(1,128)} %rows_ref.1, s32[1,1024]{1,0:T(1,128)} %cols_ref.1, s32[1,1024]{1,0:T(1,128)} %dist_ref.1), custom_call_target="tpu_custom_call" | custom-call | tf_op jit(solution)/shard_map/increment/pallas_call | solution.py:270
  47.4 1.6 %copy.9 = f32[512,64]{0,1:T(8,128)} copy(f32[512,64]{0,1:T(8,128)} %bitcast.3) | data formatting | bytes 262144

commit v6 on v5

--- a/solution.py
+++ b/solution.py
@@ -267,6 +267,7 @@
     hbm = pl.BlockSpec(memory_space=pltpu.HBM)
     each = cells // BLK
     blocks = NZ * each
+    operands = anomalies.T, innovations.T, pair_rows, pair_cols, pair_dist
     out = pl.pallas_call(
         kernel,
         out_shape=jax.ShapeDtypeStruct((columns, cells), F32),
@@ -291,10 +292,10 @@
             pltpu.SemaphoreType.REGULAR,
         ],
         compiler_params=pltpu.CompilerParams(
-            collective_id=0, has_side_effects=True, vmem_limit_bytes=56 << 20
+            collective_id=0, has_side_effects=True, vmem_limit_bytes=40 << 20
         ),
         name="increment",
-    )(pair_counts, anomalies.T, innovations.T, pair_rows, pair_cols, pair_dist)
+    )(pair_counts, *(pltpu.with_memory_space_constraint(o, pltpu.HBM) for o in operands))
     return out.T
 
 

time: 49.1 us -> 47.6 us (0.969)
  local copies, waits for them, and re-layouts: 1.57 us -> 0.66 us
  Pallas kernels: 46.7 us -> 46.2 us
    unnamed x1, local copies, waits for them, and re-layouts: 1.57 us -> 0.66 us
    pallas_call x1, Pallas kernels: 46.7 us -> 46.2 us  [local(): pl.pallas_call(kernel, out_shape=jax.ShapeDtypeStruct((columns, cells), F...]
where the time goes in v6:
time: 47.6 us; the launch traced here: 47.5 us
  Pallas kernels  46.2 us (97%)
  local copies, waits for them, and re-layouts  0.66 us (1%)
  between operations  0.66 us (1%)
    pallas_call x1, Pallas kernels, local(): pl.pallas_call(kernel, out_shape=jax.ShapeDtypeStruct((columns, cells), F...  46.2 us

profile of v6, /device:TPU:1, one launch (start us, length us, event | category | flops | bytes accessed | tf_op | source)
XLA Modules:
  0.0 47.5 jit_solution(8515383584535817161)
XLA Ops:
  0.7 46.2 %increment.1 = f32[64,512]{1,0:T(8,128)S(1)} custom-call(s32[1,1]{1,0:T(1,128)S(6)} %copy.8.count_ref, bf16[64,512]{1,0:T(8,128)(2,1)} %bitcast.4, bf16[64,512]{1,0:T(8,128)(2,1)} %bitcast.5, s32[1,1024]{1,0:T(1,128)} %rows_ref.1, s32[1,1024]{1,0:T(1,128)} %cols_ref.1, s32[1,1024]{1,0:T(1,128)} %dist_ref.1), custom_call_target="tpu_custom_call" | custom-call | tf_op jit(solution)/shard_map/increment/pallas_call | solution.py:271
  46.8 0.7 %copy.9 = f32[512,64]{0,1:T(8,128)} copy(f32[512,64]{0,1:T(8,128)S(1)} %bitcast.3) | data formatting | bytes 262144

commit v7 on v6

--- a/solution.py
+++ b/solution.py
@@ -72,7 +72,9 @@
 
     group_rows = cells // BLK
     mine = []
-    for n, (src, dst) in enumerate(((x_ref, col.at[0, r]), (v_ref, col.at[1, r]), (x_ref, row.at[z]))):
+    own_blocks = pl.ds(r * group_rows, group_rows)
+    copies_in = ((x_ref, col.at[0, own_blocks]), (v_ref, col.at[1, own_blocks]), (x_ref, row.at[z]))
+    for n, (src, dst) in enumerate(copies_in):
         for b in range(group_rows):
             mine.append(
                 pltpu.make_async_copy(
@@ -129,7 +131,7 @@
         return dev(y + (o if n else e), x + (e if n else o))
 
     def slab(n, o, e):
-        return col.at[n, place(n, o, e)]
+        return col.at[n, pl.ds(place(n, o, e) * group_rows, group_rows)]
 
     ev = {}
     sib_copies = []
@@ -161,7 +163,7 @@
     taper[0] = jnp.zeros((BLK, BLK), F32)
     for d in range(DISTS):
         taper[d + 1] = base * math.exp(-d / DIST_SCALE)
-    col_blocks = col.shape[1] * group_rows
+    col_blocks = col.shape[1]
     for c in listed:
         c.wait()
     lists[...] = slot_lists(pairs[0], pairs[1], pairs[2], count[0, 0], col_blocks)
@@ -197,8 +199,7 @@
 
     def entry(a, s):
         e = list_smem[0, a * SLOTS + s]
-        q = e & (col_blocks - 1)
-        return e // col_blocks, q // group_rows, q & (group_rows - 1)
+        return e >> (col_blocks.bit_length() - 1), e & (col_blocks - 1)
 
     def target(t):
         half = NZ // 2
@@ -219,17 +220,17 @@
                 xa = row[g, b]
                 entries = [entry(g * group_rows + b, i % turns * GROUP + n) for n in range(GROUP)]
                 products[i] = entries, [
-                    lax.dot_general(col[0, q, k], xa, tn, preferred_element_type=F32) for _, q, k in entries
+                    lax.dot_general(col[0, q], xa, tn, preferred_element_type=F32) for _, q in entries
                 ]
             if 1 <= i <= steps:
                 entries, prods = products.pop(i - 1)
                 tapered[i - 1] = entries, jnp.concatenate(
-                    [(p * taper[d]).astype(BF16) for p, (d, _, _) in zip(prods, entries)], axis=0
+                    [(p * taper[d]).astype(BF16) for p, (d, _) in zip(prods, entries)], axis=0
                 )
             if i >= 2:
                 b, turn = divmod(i - 2, turns)
                 entries, weights = tapered.pop(i - 2)
-                vb = jnp.concatenate([col[1, q, k] for _, q, k in entries], axis=1)
+                vb = jnp.concatenate([col[1, q] for _, q in entries], axis=1)
                 term = jnp.dot(vb, weights, preferred_element_type=F32)
                 sums[b] = term if turn == 0 else sums[b] + term
                 if turn == turns - 1:
@@ -276,7 +277,7 @@
         scratch_shapes=[
             pltpu.SMEM(pair_counts.shape, jnp.int32),
             pltpu.VMEM((3,) + pair_rows.shape, jnp.int32),
-            pltpu.VMEM((2, n_rows, each, members, BLK), BF16),
+            pltpu.VMEM((2, n_rows * each, members, BLK), BF16),
             pltpu.VMEM((NZ, each, members, BLK), BF16),
             pltpu.VMEM((DISTS + 1, BLK, BLK), F32),
             pltpu.VMEM((1, blocks * SLOTS), jnp.int32),

time: 47.6 us -> 47.1 us (0.989)
  Pallas kernels: 46.2 us -> 45.6 us
    pallas_call x1, Pallas kernels: 46.2 us -> 45.6 us  [local(): pl.pallas_call(kernel, out_shape=jax.ShapeDtypeStruct((columns, cells), F...]
where the time goes in v7:
time: 47.1 us; the launch traced here: 47 us
  Pallas kernels  45.6 us (97%)
  local copies, waits for them, and re-layouts  0.66 us (1%)
  between operations  0.66 us (1%)
    pallas_call x1, Pallas kernels, local(): pl.pallas_call(kernel, out_shape=jax.ShapeDtypeStruct((columns, cells), F...  45.6 us

profile of v7, /device:TPU:1, one launch (start us, length us, event | category | flops | bytes accessed | tf_op | source)
XLA Modules:
  0.0 47.0 jit_solution(14429593499781966361)
XLA Ops:
  0.7 45.6 %increment.1 = f32[64,512]{1,0:T(8,128)S(1)} custom-call(s32[1,1]{1,0:T(1,128)S(6)} %copy.8.count_ref, bf16[64,512]{1,0:T(8,128)(2,1)} %bitcast.4, bf16[64,512]{1,0:T(8,128)(2,1)} %bitcast.5, s32[1,1024]{1,0:T(1,128)} %rows_ref.1, s32[1,1024]{1,0:T(1,128)} %cols_ref.1, s32[1,1024]{1,0:T(1,128)} %dist_ref.1), custom_call_target="tpu_custom_call" | custom-call | tf_op jit(solution)/shard_map/increment/pallas_call | solution.py:272
  46.3 0.7 %copy.9 = f32[512,64]{0,1:T(8,128)} copy(f32[512,64]{0,1:T(8,128)S(1)} %bitcast.3) | data formatting | bytes 262144

commit v8 on v7

--- a/solution.py
+++ b/solution.py
@@ -69,6 +69,16 @@
         return (lax.rem(yy + NY, NY) * NX + lax.rem(xx + NX, NX)) * 2 + core
 
     sib = r + 1 - 2 * core
+
+    barrier = pltpu.get_barrier_semaphore()
+    peers = [(sib, z)]
+    peers += [(dev(y, x + d), z) for d in RING] + [(dev(y + d, x), z) for d in RING]
+    for peer in peers:
+        pl.semaphore_signal(barrier, inc=1, device_id=peer, device_id_type=MESH)
+    for k in range(1, NZ):
+        @pl.when(z + k < NZ)
+        def _():
+            pl.semaphore_signal(barrier, inc=1, device_id=(r, lax.rem(z + k, NZ)), device_id_type=MESH)
 
     group_rows = cells // BLK
     mine = []
@@ -88,16 +98,6 @@
         listed.append(pltpu.make_async_copy(ref, pairs.at[n], local_sem.at[3 * group_rows + 1 + n]))
     for c in listed:
         c.start()
-
-    barrier = pltpu.get_barrier_semaphore()
-    peers = [(sib, z)]
-    peers += [(dev(y, x + d), z) for d in RING] + [(dev(y + d, x), z) for d in RING]
-    for peer in peers:
-        pl.semaphore_signal(barrier, inc=1, device_id=peer, device_id_type=MESH)
-    for k in range(1, NZ):
-        @pl.when(z + k < NZ)
-        def _():
-            pl.semaphore_signal(barrier, inc=1, device_id=(r, lax.rem(z + k, NZ)), device_id_type=MESH)
 
     for c in mine:
         c.wait()

time: 47.1 us -> 47.1 us (level)
  no operation moved by 1% of the time
where the time goes in v8:
time: 47.1 us; the launch traced here: 46.9 us
  Pallas kernels  45.6 us (97%)
  local copies, waits for them, and re-layouts  0.66 us (1%)
  between operations  0.66 us (1%)
    pallas_call x1, Pallas kernels, local(): pl.pallas_call(kernel, out_shape=jax.ShapeDtypeStruct((columns, cells), F...  45.6 us

profile of v8, /device:TPU:1, one launch (start us, length us, event | category | flops | bytes accessed | tf_op | source)
XLA Modules:
  0.0 46.9 jit_solution(12605876731642056183)
XLA Ops:
  0.7 45.6 %increment.1 = f32[64,512]{1,0:T(8,128)S(1)} custom-call(s32[1,1]{1,0:T(1,128)S(6)} %copy.8.count_ref, bf16[64,512]{1,0:T(8,128)(2,1)} %bitcast.4, bf16[64,512]{1,0:T(8,128)(2,1)} %bitcast.5, s32[1,1024]{1,0:T(1,128)} %rows_ref.1, s32[1,1024]{1,0:T(1,128)} %cols_ref.1, s32[1,1024]{1,0:T(1,128)} %dist_ref.1), custom_call_target="tpu_custom_call" | custom-call | tf_op jit(solution)/shard_map/increment/pallas_call | solution.py:272
  46.3 0.7 %copy.9 = f32[512,64]{0,1:T(8,128)} copy(f32[512,64]{0,1:T(8,128)S(1)} %bitcast.3) | data formatting | bytes 262144
